TPU v7x, 128 devices: a whole 4x4x4 slice. The times are simulated.
128 devices in a mesh: dp: 8 (over z, core), expert: 16 (over y, x).
Axes of the slice: x: 4, y: 4, z: 4, core: 2. Of those that a mesh axis runs over, the one named last changes fastest.
Arguments:
- inputs: bfloat16 [16384, 2048], P(('dp', 'expert')), may hold values from -6 to 6
- out_grad: bfloat16 [16384, 2048], P(('dp', 'expert')), may hold values from -6 to 6
- combine: float32 [16384, 8], P(('dp', 'expert')), may hold values from 0 to 1, as said below
- routes: int32 [16384, 8], P(('dp', 'expert')), may hold values from 0 to 63, all different within a row; in each aligned block of 128 rows (0 to 127, 128 to 255, ...) at most 24 rows name the same one
- saved_hidden: bfloat16 [8, 64, 16, 24, 768], P('dp', 'expert'), may hold values from -6 to 6
- down_weight: bfloat16 [64, 2048, 768], P('expert'), may hold values from -0.21875 to 0.21875
- router_weight: bfloat16 [64, 2048], replicated, may hold values from -0.125 to 0.125
Outputs:
- hidden_grad: bfloat16 [8, 64, 16, 24, 768], P('dp', 'expert')
- down_grad: bfloat16 [64, 2048, 768], P('expert', 'dp')
- input_grad: bfloat16 [16384, 2048], P(('dp', 'expert'))
- router_grad: float32 [64, 2048], replicated
Inputs may be any that keep to these rules, and one draw needn't show every extreme that they name: `routes`: each token names 8 different experts; among the 128 tokens of one device no expert is named by more than 24 tokens, a bound that some block reaches. `combine`: each token's 8 weights are positive and sum to one.
All inputs are finite; a program needn't handle non-finite values.
Results may differ from a plain program's by a relative error of at most 0.017.
Values may be sent and summed in bfloat16 or wider, within the bound.
A program may use at most 128 MiB of HBM per device.

v0:
```python
import jax
import jax.numpy as jnp
from jax import lax
from jax.sharding import PartitionSpec as P


def make_marks(block_routes, total_experts):
    return block_routes[:, :, None] == jnp.arange(total_experts, dtype=jnp.int32)[None, None, :]


def slot_positions(route_marks):
    counts = jnp.sum(route_marks.astype(jnp.bfloat16), axis=1)
    token_order = jnp.arange(route_marks.shape[0], dtype=jnp.int32)
    earlier = (token_order[None, :] < token_order[:, None]).astype(jnp.bfloat16)
    before = jnp.dot(earlier, counts, preferred_element_type=jnp.float32)
    picked = jnp.sum(jnp.where(route_marks, before[:, None, :], 0.0), axis=2)
    return picked.astype(jnp.int32)


def pack_rows(scaled, lane_index, owner_slot, positions, local_experts, groups, capacity):
    width = scaled.shape[-1]
    flat_index = (owner_slot * groups + lane_index) * capacity + positions
    zero_rows = jnp.zeros((local_experts * groups * capacity, width), jnp.bfloat16)
    filled = zero_rows.at[flat_index.reshape(-1)].set(scaled.reshape(-1, width))
    return filled.reshape(local_experts, groups, capacity, width)


def local(inputs, out_grad, combine, routes, saved_hidden, down_weight, router_weight):
    token_count, width = out_grad.shape
    local_experts = down_weight.shape[0]
    total_experts = router_weight.shape[0]
    groups = lax.axis_size("expert")
    capacity = saved_hidden.shape[3]
    hidden_width = saved_hidden.shape[4]
    route_marks = make_marks(routes, total_experts)
    positions = slot_positions(route_marks)
    owner_dev = routes // local_experts
    owner_slot = routes % local_experts
    scaled = (combine[:, :, None] * out_grad[:, None, :].astype(jnp.float32)).astype(jnp.bfloat16)
    packed = pack_rows(scaled, owner_dev, owner_slot, positions, local_experts, groups, capacity)
    received = lax.all_to_all(packed, "expert", split_axis=1, concat_axis=1, tiled=True)
    hidden_local = saved_hidden[0]
    products_list = []
    hidden_list = []
    weight_terms = []
    for expert in range(local_experts):
        slot_rows = received[expert].reshape(groups * capacity, width)
        slot_acts = hidden_local[expert].reshape(groups * capacity, hidden_width)
        weight = down_weight[expert]
        recomputed = lax.dot_general(
            slot_acts, weight, (((1,), (1,)), ((), ())), preferred_element_type=jnp.float32
        )
        products_list.append(jnp.sum(recomputed * slot_rows.astype(jnp.float32), axis=1))
        hidden_list.append(
            jnp.dot(slot_rows, weight, preferred_element_type=jnp.float32).astype(jnp.bfloat16)
        )
        weight_terms.append(
            lax.dot_general(
                slot_rows, slot_acts, (((0,), (0,)), ((), ())), preferred_element_type=jnp.float32
            )
        )
    down_grad = lax.psum_scatter(
        jnp.stack(weight_terms).astype(jnp.bfloat16), "dp", scatter_dimension=1, tiled=True
    )
    hidden_grad = jnp.stack(hidden_list).reshape(1, local_experts, groups, capacity, hidden_width)
    slot_products = jnp.stack(products_list).reshape(local_experts, groups, capacity)
    returned = lax.all_to_all(slot_products, "expert", split_axis=1, concat_axis=1, tiled=True)
    pair_index = (owner_slot * groups + owner_dev) * capacity + positions
    pair_sums = returned.reshape(-1)[pair_index]
    logit_grad = pair_sums - combine * jnp.sum(pair_sums, axis=1, keepdims=True)
    dense_grad = jnp.sum(jnp.where(route_marks, logit_grad[:, :, None], 0.0), axis=1).astype(
        jnp.bfloat16
    )
    input_grad = jnp.dot(dense_grad, router_weight, preferred_element_type=jnp.float32).astype(
        jnp.bfloat16
    )
    router_part = lax.dot_general(
        dense_grad, inputs, (((0,), (0,)), ((), ())), preferred_element_type=jnp.float32
    )
    router_grad = lax.psum(router_part, ("dp", "expert"))
    return (hidden_grad, down_grad, input_grad, router_grad)


def solution(mesh):
    placed = (
        P(("dp", "expert"), None),
        P(("dp", "expert"), None),
        P(("dp", "expert"), None),
        P(("dp", "expert"), None),
        P("dp", "expert", None, None, None),
        P("expert", None, None),
        P(),
    )
    return jax.shard_map(
        local,
        mesh=mesh,
        in_specs=placed,
        out_specs=(
            P("dp", "expert", None, None, None),
            P("expert", "dp", None),
            P(("dp", "expert"), None),
            P(),
        ),
        check_vma=False,
    )
```

profile of v0, /device:TPU:1, one launch (start us, length us, event | category | flops | bytes accessed | tf_op | source)
XLA Modules:
  0.0 366.2 jit_solution(16921963926218966697)
XLA Ops:
  12.6 10.6 %scatter_custom_fusion = bf16[1536,2048]{1,0:T(8,128)(2,1)} fusion(s32[1024]{0:T(1024)S(1)} %bitcast.110, f32[128,2048]{1,0:T(8,128)S(1)} %convert_element_type.50, f32[1024]{0:T(1024)S(1)} %mul.48, bf16[]{:T(256)} %constant.31.clone.1), kind=kCustom, calls=%fused_computation.5 | custom fusion | flops 4194304 | bytes 7344130 | tf_op jit(solution)/shard_map/scatter | solution.py:24
  23.2 6.6 %copy.47 = bf16[4,16,24,2048]{3,2,0,1:T(8,128)(2,1)} copy(bf16[4,16,24,2048]{3,2,1,0:T(8,128)(2,1)} %bitcast.85) | data formatting | bytes 12582912 | tf_op jit(solution)/shard_map/reshape | solution.py:25
  29.8 7.8 %all-to-all-start = ((bf16[4,16,24,2048]{3,2,0,1:T(8,128)(2,1)}), bf16[4,16,24,2048]{3,2,0,1:T(8,128)(2,1)}, u32[]{:S(2)}, u32[]{:S(2)}) async-start(bf16[4,16,24,2048]{3,2,0,1:T(8,128)(2,1)} %copy.47), calls=%async_computation | async-start | bytes 12582912 | tf_op jit(solution)/shard_map/all_to_all | solution.py:41
  39.0 90.8 %all-to-all-done = bf16[4,16,24,2048]{3,2,0,1:T(8,128)(2,1)} async-done(((bf16[4,16,24,2048]{3,2,0,1:T(8,128)(2,1)}), bf16[4,16,24,2048]{3,2,0,1:T(8,128)(2,1)}, u32[]{:S(2)}, u32[]{:S(2)}) %all-to-all-start) | async-done | bytes 6291488 | tf_op jit(solution)/shard_map/all_to_all | solution.py:41
  129.9 4.8 %fusion.69 = (bf16[1,16,24,2048]{3,2,0,1:T(8,128)(2,1)S(1)}, bf16[1,16,24,2048]{3,2,0,1:T(8,128)(2,1)}, bf16[1,16,24,2048]{3,2,0,1:T(8,128)(2,1)S(1)}, bf16[1,16,24,2048]{3,2,0,1:T(8,128)(2,1)S(1)}) fusion(bf16[4,16,24,2048]{3,2,0,1:T(8,128)(2,1)} %all-to-all-done), kind=kLoop, calls=%fused_computation.80 | loop fusion | bytes 12582912 | tf_op jit(solution)/shard_map/slice | solution.py:47
  134.7 3.5 fusion.23
  138.2 3.6 multiply_reduce_fusion.2
  141.9 1.5 multiply_reduce_fusion.1
  143.4 3.5 fusion.24
  146.9 1.5 multiply_reduce_fusion.3
  148.4 3.5 fusion.22
  152.2 3.9 %multiply_reduce_fusion = f32[384]{0:T(512)S(1)} fusion(bf16[384,2048]{1,0:T(8,128)(2,1)} %bitcast.95, bf16[384,768]{1,0:T(8,128)(2,1)S(1)} %bitcast.98, bf16[4,2048,768]{2,1,0:T(8,128)(2,1)} %param.12), kind=kOutput, calls=%fused_computation.28 | convolution fusion | flops 1210318464 | bytes 5309952 | tf_op jit(solution)/shard_map/dot_general | solution.py:50
  156.9 5.4 %all-to-all-start.1 = ((f32[4,16,24]{2,0,1:T(4,128)}), f32[4,16,24]{2,0,1:T(4,128)S(1)}, u32[]{:S(2)}, u32[]{:S(2)}) async-start(f32[4,16,24]{2,0,1:T(4,128)} %pad_maximum_fusion.2), calls=%async_computation.2 | async-start | bytes 65536 | tf_op jit(solution)/shard_map/all_to_all | solution.py:67
  162.6 4.9 %fusion.25 = bf16[1,2048,768]{2,1,0:T(8,128)(2,1)} fusion(bf16[384,2048]{1,0:T(8,128)(2,1)} %bitcast.96, bf16[384,768]{1,0:T(8,128)(2,1)S(1)} %bitcast.99), kind=kOutput, calls=%fused_computation.36 | convolution fusion | flops 1209532416 | bytes 5308416 | tf_op jit(solution)/shard_map/dot_general | solution.py:58
  167.5 1.3 all-to-all-done.1
  168.8 6.2 %gather_fusion = f32[1024]{0:T(1024)S(1)} fusion(f32[1536]{0:T(1024)S(1)} %reshape.84, s32[1024]{0:T(1024)S(1)} %broadcast_clamp_fusion), kind=kCustom, calls=%fused_computation | custom fusion | bytes 12288 | tf_op jit(solution)/shard_map/gather | solution.py:69
  176.5 10.7 %pad_maximum_fusion = bf16[4,2048,768]{2,1,0:T(8,128)(2,1)} fusion(bf16[1,2048,768]{2,1,0:T(8,128)(2,1)} %fusion.25, bf16[1,2048,768]{2,1,0:T(8,128)(2,1)} %fusion.24, bf16[1,2048,768]{2,1,0:T(8,128)(2,1)} %fusion.23, bf16[1,2048,768]{2,1,0:T(8,128)(2,1)} %fusion.22), kind=kLoop, calls=%fused_computation.2 | loop fusion | flops 18874368 | bytes 25165824 | tf_op jit(solution)/shard_map/stack | solution.py:63
  187.2 3.9 %fusion.51 = bf16[384,768]{1,0:T(8,128)(2,1)S(1)} fusion(bf16[384,2048]{1,0:T(8,128)(2,1)} %bitcast.97, bf16[4,2048,768]{2,1,0:T(8,128)(2,1)} %param.12), kind=kOutput, calls=%fused_computation.50 | convolution fusion | flops 1208254464 | bytes 5308416 | tf_op jit(solution)/shard_map/dot_general | solution.py:55
  191.1 3.4 fusion.42
  194.6 3.3 fusion.48
  197.9 4.1 %fusion.45 = bf16[384,768]{1,0:T(8,128)(2,1)S(1)} fusion(bf16[384,2048]{1,0:T(8,128)(2,1)S(1)} %bitcast.88, bf16[4,2048,768]{2,1,0:T(8,128)(2,1)} %param.12), kind=kOutput, calls=%fused_computation.48 | convolution fusion | flops 1208254464 | bytes 5308416 | tf_op jit(solution)/shard_map/dot_general | solution.py:55
  202.0 1.7 pad_maximum_fusion.1
  204.9 152.0 %all-reduce.2.cloned.1.call-done = f32[64,2048]{1,0:T(8,128)} async-done(((f32[64,2048]{1,0:T(8,128)}), f32[64,2048]{1,0:T(8,128)}) %all-reduce.2.cloned.1.call-update) | async-done | bytes 524304 | tf_op jit(solution)/shard_map/psum | solution.py:80
  356.9 1.9 copy.52
  (64 shorter events, 10.0 us)
Async XLA Ops:
  8.0 167.4 %copy-start = (bf16[128,2048]{1,0:T(8,128)(2,1)S(1)}, bf16[128,2048]{1,0:T(8,128)(2,1)}, u32[]{:S(2)}) copy-start(bf16[128,2048]{1,0:T(8,128)(2,1)} %param.7) | copy-start | bytes 1572868
  29.8 8.0 %copy-start.1 = (bf16[1,4,16,24,768]{4,3,2,1,0:T(8,128)(2,1)S(1)}, bf16[1,4,16,24,768]{4,3,2,1,0:T(8,128)(2,1)}, u32[]{:S(2)}) copy-start(bf16[1,4,16,24,768]{4,3,2,1,0:T(8,128)(2,1)} %param.11) | copy-start | bytes 7077892
  29.8 100.1 %all-to-all-start = ((bf16[4,16,24,2048]{3,2,0,1:T(8,128)(2,1)}), bf16[4,16,24,2048]{3,2,0,1:T(8,128)(2,1)}, u32[]{:S(2)}, u32[]{:S(2)}) async-start(bf16[4,16,24,2048]{3,2,0,1:T(8,128)(2,1)} %copy.47), calls=%async_computation | async-start | bytes 12582912 | tf_op jit(solution)/shard_map/all_to_all | solution.py:41
  39.0 95.7 %copy-start.8 = (bf16[1,1,16,24,768]{4,3,2,1,0:T(8,128)(2,1)S(1)}, bf16[1,1,16,24,768]{4,3,2,1,0:T(8,128)(2,1)}, u32[]{:S(2)}) copy-start(bf16[1,1,16,24,768]{4,3,2,1,0:T(8,128)(2,1)} %get-tuple-element.11) | copy-start | bytes 1769476
  129.9 11.9 %slice-start = ((s8[12582912]{0:T(1024)(128)(4,1)}), s8[4194304]{0:T(1024)(128)(4,1)S(1)}, s32[]{:S(2)}) async-start(s8[12582912]{0:T(1024)(128)(4,1)} %bitcast.111), calls=%async_computation.5 | async-start | bytes 8388608
  129.9 11.9 %slice-start.1 = ((s8[12582912]{0:T(1024)(128)(4,1)}), s8[4194304]{0:T(1024)(128)(4,1)S(1)}, s32[]{:S(2)}) async-start(s8[12582912]{0:T(1024)(128)(4,1)} %bitcast.111), calls=%async_computation.6 | async-start | bytes 8388608
  134.7 8.7 %copy-start.2 = (bf16[1,16,24,2048]{3,2,0,1:T(8,128)(2,1)}, bf16[1,16,24,2048]{3,2,0,1:T(8,128)(2,1)S(1)}, u32[]{:S(2)}) copy-start(bf16[1,16,24,2048]{3,2,0,1:T(8,128)(2,1)S(1)} %get-tuple-element.8) | copy-start | bytes 4718596
  134.7 13.7 %copy-start.4 = (bf16[1,16,24,2048]{3,2,0,1:T(8,128)(2,1)}, bf16[1,16,24,2048]{3,2,0,1:T(8,128)(2,1)S(1)}, u32[]{:S(2)}) copy-start(bf16[1,16,24,2048]{3,2,0,1:T(8,128)(2,1)S(1)} %get-tuple-element.6) | copy-start | bytes 4718596
  138.2 3.6 copy-start.7
  138.2 3.6 slice-start.2
  143.4 3.5 copy-start.6
  156.9 11.8 %all-to-all-start.1 = ((f32[4,16,24]{2,0,1:T(4,128)}), f32[4,16,24]{2,0,1:T(4,128)S(1)}, u32[]{:S(2)}, u32[]{:S(2)}) async-start(f32[4,16,24]{2,0,1:T(4,128)} %pad_maximum_fusion.2), calls=%async_computation.2 | async-start | bytes 65536 | tf_op jit(solution)/shard_map/all_to_all | solution.py:67
  162.3 194.6 %all-reduce.2.cloned.1.call-start = ((), (), s32[]{:S(2)}) async-start(), calls=%async_computation.4 | async-start | bytes 1048576 | tf_op jit(solution)/shard_map/psum | solution.py:80
  168.8 6.5 %copy-start.11 = (f32[128,8]{0,1:T(8,128)S(1)}, f32[128,8]{0,1:T(8,128)}, u32[]{:S(2)}) copy-start(f32[128,8]{0,1:T(8,128)} %param.9) | copy-start | bytes 12292
  168.8 6.5 %copy-start.10 = (s32[128,8]{0,1:T(8,128)S(1)}, s32[128,8]{0,1:T(8,128)}, u32[]{:S(2)}) copy-start(s32[128,8]{0,1:T(8,128)} %param.10) | copy-start | bytes 12292
  176.4 180.5 %reduce-scatter.2.cloned.1.call-start = ((), (), s32[]{:S(2)}) async-start(), calls=%async_computation.3 | async-start | bytes 14155776 | tf_op jit(solution)/shard_map/reduce_scatter | solution.py:62
  187.2 3.9 %copy-start.5 = (bf16[1,16,24,2048]{3,2,0,1:T(8,128)(2,1)S(1)}, bf16[1,16,24,2048]{3,2,0,1:T(8,128)(2,1)}, u32[]{:S(2)}) copy-start(bf16[1,16,24,2048]{3,2,0,1:T(8,128)(2,1)} %copy-done.4) | copy-start | bytes 4718596
  191.1 3.5 copy-start.3
  202.0 1.7 copy-start.9
Sparse Core Ops, SparseCore 0:
  176.5 180.2 all-reduce.1
Sparse Core Ops, SparseCore 1:
  187.3 75.3 reduce-scatter.1
where the time goes:
time: 367 us; the launch traced here: 366 us
  waiting for transfers between devices  244 us (66%)
  matrix products  43 us (12%)
  other arithmetic  27.2 us (7%)
  local copies, waits for them, and re-layouts  22.6 us (6%)
  between operations  15.8 us (4%)
  starting transfers between devices  13.5 us (4%)
    psum x1, waiting for transfers between devices, local(): router_grad = lax.psum(router_part, ('dp', 'expert'))  152 us
    all_to_all x1, waiting for transfers between devices, local(): lax.all_to_all(packed, 'expert', split_axis=1, concat_axis=1, tiled=True)  90.8 us
    dot_general x4, matrix products, local(): lax.dot_general(slot_rows, slot_acts, (((0,), (0,)), ((), ())), preferred...  15.5 us
    dot_general x4, matrix products, local(): jnp.dot(slot_rows, weight, preferred_element_type=jnp.float32)  14.8 us
    another operation x1, other arithmetic, local(): jnp.stack(weight_terms).astype(jnp.bfloat16)  10.7 us
    scatter x1, other arithmetic, pack_rows(): filled = zero_rows.at[flat_index.reshape(-1)].set(scaled.reshape(-1, width))  10.6 us
    dot_general x4, matrix products, local(): lax.dot_general(slot_acts, weight, (((1,), (1,)), ((), ())), preferred_el...  10.5 us
    all_to_all x1, starting transfers between devices, local(): lax.all_to_all(packed, 'expert', split_axis=1, concat_axis=1, tiled=True)  7.77 us
  transfers between devices with their start and end apart: 4, of which 3 were waited for; matrix products, arithmetic and copies ran while one was open for 9% of the time, Pallas kernels for 0%

commit v1 on v0

--- a/solution.py
+++ b/solution.py
@@ -77,7 +77,7 @@
     router_part = lax.dot_general(
         dense_grad, inputs, (((0,), (0,)), ((), ())), preferred_element_type=jnp.float32
     )
-    router_grad = lax.psum(router_part, ("dp", "expert"))
+    router_grad = jnp.sum(lax.all_gather(router_part, ("dp", "expert")), axis=0)
     return (hidden_grad, down_grad, input_grad, router_grad)
 
 

time: 367 us -> 406 us (1.11)
  waiting for transfers between devices: 244 us -> 269 us
  other arithmetic: 27.2 us -> 44.3 us
    all_gather x0 -> x1, waiting for transfers between devices: none -> 172 us  [local(): router_grad = jnp.sum(lax.all_gather(router_part, ('dp', 'expert')), axis=0)]
    psum x1 -> x0, waiting for transfers between devices: 152 us -> none  [local(): router_grad = lax.psum(router_part, ('dp', 'expert'))]
    reduce_sum x0 -> x1, other arithmetic: none -> 21.7 us  [local(): router_grad = jnp.sum(lax.all_gather(router_part, ('dp', 'expert')), axis=0)]
    dot_general x4, matrix products: 15.5 us -> 9.08 us  [local(): lax.dot_general(slot_rows, slot_acts, (((0,), (0,)), ((), ())), preferred...]
    all_to_all x1, waiting for transfers between devices: 1.26 us -> 6.39 us  [local(): lax.all_to_all(slot_products, 'expert', split_axis=1, concat_axis=1, tile...]
    another operation x1, other arithmetic: 10.7 us -> 6.09 us  [local(): jnp.stack(weight_terms).astype(jnp.bfloat16)]
    dot_general x4, matrix products: 10.5 us -> 14.8 us  [local(): lax.dot_general(slot_acts, weight, (((1,), (1,)), ((), ())), preferred_el...]
  transfers between devices with their start and end apart: 4 -> 4, of which waited for: 3 -> 3; matrix products, arithmetic and copies ran while one was open for 9% -> 14% of each run, Pallas kernels for 0% -> 0%
where the time goes in v1:
time: 406 us
  waiting for transfers between devices  269 us (66%)
  other arithmetic  44.3 us (11%)
  matrix products  40.4 us (10%)
  local copies, waits for them, and re-layouts  22.5 us (6%)
  between operations  15.8 us (4%)
  starting transfers between devices  13.5 us (3%)
    all_gather x1, waiting for transfers between devices, local(): router_grad = jnp.sum(lax.all_gather(router_part, ('dp', 'expert')), axis=0)  172 us
    all_to_all x1, waiting for transfers between devices, local(): lax.all_to_all(packed, 'expert', split_axis=1, concat_axis=1, tiled=True)  90.8 us
    reduce_sum x1, other arithmetic, local(): router_grad = jnp.sum(lax.all_gather(router_part, ('dp', 'expert')), axis=0)  21.7 us
    dot_general x4, matrix products, local(): lax.dot_general(slot_acts, weight, (((1,), (1,)), ((), ())), preferred_el...  14.8 us
    dot_general x4, matrix products, local(): jnp.dot(slot_rows, weight, preferred_element_type=jnp.float32)  14.2 us
    scatter x1, other arithmetic, pack_rows(): filled = zero_rows.at[flat_index.reshape(-1)].set(scaled.reshape(-1, width))  10.6 us
    dot_general x4, matrix products, local(): lax.dot_general(slot_rows, slot_acts, (((0,), (0,)), ((), ())), preferred...  9.08 us
  transfers between devices with their start and end apart: 4, of which 3 were waited for; matrix products, arithmetic and copies ran while one was open for 14% of the time, Pallas kernels for 0%

profile of v1, /device:TPU:1, one launch (start us, length us, event | category | flops | bytes accessed | tf_op | source)
XLA Modules:
  0.0 405.7 jit_solution(11098932272805189669)
XLA Ops:
  12.6 10.6 %scatter_custom_fusion = bf16[1536,2048]{1,0:T(8,128)(2,1)} fusion(s32[1024]{0:T(1024)S(1)} %bitcast.110, f32[128,2048]{1,0:T(8,128)S(1)} %convert_element_type.50, f32[1024]{0:T(1024)S(1)} %mul.48, bf16[]{:T(256)} %constant.31.clone.1), kind=kCustom, calls=%fused_computation.5 | custom fusion | flops 4194304 | bytes 7344130 | tf_op jit(solution)/shard_map/scatter | solution.py:24
  23.2 6.6 %copy.47 = bf16[4,16,24,2048]{3,2,0,1:T(8,128)(2,1)} copy(bf16[4,16,24,2048]{3,2,1,0:T(8,128)(2,1)} %bitcast.85) | data formatting | bytes 12582912 | tf_op jit(solution)/shard_map/reshape | solution.py:25
  29.8 7.8 %all-to-all-start = ((bf16[4,16,24,2048]{3,2,0,1:T(8,128)(2,1)}), bf16[4,16,24,2048]{3,2,0,1:T(8,128)(2,1)}, u32[]{:S(2)}, u32[]{:S(2)}) async-start(bf16[4,16,24,2048]{3,2,0,1:T(8,128)(2,1)} %copy.47), calls=%async_computation | async-start | bytes 12582912 | tf_op jit(solution)/shard_map/all_to_all | solution.py:41
  39.0 90.8 %all-to-all-done = bf16[4,16,24,2048]{3,2,0,1:T(8,128)(2,1)} async-done(((bf16[4,16,24,2048]{3,2,0,1:T(8,128)(2,1)}), bf16[4,16,24,2048]{3,2,0,1:T(8,128)(2,1)}, u32[]{:S(2)}, u32[]{:S(2)}) %all-to-all-start) | async-done | bytes 6291488 | tf_op jit(solution)/shard_map/all_to_all | solution.py:41
  129.9 5.4 %fusion.69 = (bf16[1,16,24,2048]{3,2,0,1:T(8,128)(2,1)S(1)}, bf16[1,16,24,2048]{3,2,0,1:T(8,128)(2,1)S(1)}, bf16[1,16,24,2048]{3,2,0,1:T(8,128)(2,1)}, bf16[1,16,24,2048]{3,2,0,1:T(8,128)(2,1)}) fusion(bf16[4,16,24,2048]{3,2,0,1:T(8,128)(2,1)} %all-to-all-done), kind=kLoop, calls=%fused_computation.80 | loop fusion | bytes 12582912 | tf_op jit(solution)/shard_map/slice | solution.py:47
  136.5 3.4 multiply_reduce_fusion
  140.0 4.1 %multiply_reduce_fusion.1 = f32[384]{0:T(512)S(1)} fusion(bf16[384,2048]{1,0:T(8,128)(2,1)} %bitcast.92, bf16[384,768]{1,0:T(8,128)(2,1)} %bitcast.102, bf16[4,2048,768]{2,1,0:T(8,128)(2,1)} %param.12), kind=kOutput, calls=%fused_computation.29 | convolution fusion | flops 1210318464 | bytes 5309952 | tf_op jit(solution)/shard_map/dot_general | solution.py:50
  144.2 3.9 multiply_reduce_fusion.2
  148.2 3.4 multiply_reduce_fusion.3
  152.3 5.4 %all-to-all-start.1 = ((f32[4,16,24]{2,0,1:T(4,128)}), f32[4,16,24]{2,0,1:T(4,128)S(1)}, u32[]{:S(2)}, u32[]{:S(2)}) async-start(f32[4,16,24]{2,0,1:T(4,128)} %pad_maximum_fusion.2), calls=%async_computation.2 | async-start | bytes 65536 | tf_op jit(solution)/shard_map/all_to_all | solution.py:67
  157.8 6.4 %all-to-all-done.1 = f32[4,16,24]{2,0,1:T(4,128)S(1)} async-done(((f32[4,16,24]{2,0,1:T(4,128)}), f32[4,16,24]{2,0,1:T(4,128)S(1)}, u32[]{:S(2)}, u32[]{:S(2)}) %all-to-all-start.1) | async-done | bytes 6176 | tf_op jit(solution)/shard_map/all_to_all | solution.py:67
  164.3 6.2 %gather_fusion = f32[1024]{0:T(1024)S(1)} fusion(f32[1536]{0:T(1024)S(1)} %reshape.84, s32[1024]{0:T(1024)S(1)} %broadcast_clamp_fusion), kind=kCustom, calls=%fused_computation | custom fusion | bytes 12288 | tf_op jit(solution)/shard_map/gather | solution.py:69
  172.2 3.5 fusion.25
  175.7 1.8 fusion.24
  177.6 1.9 fusion.23
  179.4 1.9 fusion.22
  181.3 6.1 %pad_maximum_fusion = bf16[4,2048,768]{2,1,0:T(8,128)(2,1)} fusion(bf16[1,2048,768]{2,1,0:T(8,128)(2,1)S(1)} %fusion.25, bf16[1,2048,768]{2,1,0:T(8,128)(2,1)S(1)} %fusion.24, bf16[1,2048,768]{2,1,0:T(8,128)(2,1)S(1)} %fusion.23, bf16[1,2048,768]{2,1,0:T(8,128)(2,1)S(1)} %fusion.22), kind=kLoop, calls=%fused_computation.2 | loop fusion | flops 18874368 | bytes 25165824 | tf_op jit(solution)/shard_map/stack | solution.py:63
  187.4 3.9 fusion.51
  191.3 3.4 fusion.48
  194.8 3.3 fusion.45
  198.1 3.6 fusion.42
  201.7 1.7 pad_maximum_fusion.1
  204.5 172.0 %all-gather.3.cloned.1.call-done = f32[8192,2048]{1,0:T(8,128)} async-done(((f32[64,2048]{1,0:T(8,128)}), f32[8192,2048]{1,0:T(8,128)}) %all-gather.3.cloned.1.call-update) | async-done | bytes 67108880 | tf_op jit(solution)/shard_map/all_gather | solution.py:80
  376.6 21.7 %reduce_sum.92 = f32[64,2048]{1,0:T(8,128)} reduce(f32[128,64,2048]{2,1,0:T(8,128)} %bitcast.23, f32[]{:T(128)} %constant.40.clone.1), dimensions={0}, to_apply=%region_10.11 | reduce | flops 16646144 | bytes 67633152 | tf_op jit(solution)/shard_map/reduce_sum | solution.py:80
  (61 shorter events, 11.2 us)
Async XLA Ops:
  8.0 162.8 %copy-start = (bf16[128,2048]{1,0:T(8,128)(2,1)S(1)}, bf16[128,2048]{1,0:T(8,128)(2,1)}, u32[]{:S(2)}) copy-start(bf16[128,2048]{1,0:T(8,128)(2,1)} %param.7) | copy-start | bytes 1572868
  29.8 8.0 %copy-start.2 = (bf16[1,4,16,24,768]{4,3,2,1,0:T(8,128)(2,1)S(1)}, bf16[1,4,16,24,768]{4,3,2,1,0:T(8,128)(2,1)}, u32[]{:S(2)}) copy-start(bf16[1,4,16,24,768]{4,3,2,1,0:T(8,128)(2,1)} %param.11) | copy-start | bytes 7077892
  29.8 100.1 %all-to-all-start = ((bf16[4,16,24,2048]{3,2,0,1:T(8,128)(2,1)}), bf16[4,16,24,2048]{3,2,0,1:T(8,128)(2,1)}, u32[]{:S(2)}, u32[]{:S(2)}) async-start(bf16[4,16,24,2048]{3,2,0,1:T(8,128)(2,1)} %copy.47), calls=%async_computation | async-start | bytes 12582912 | tf_op jit(solution)/shard_map/all_to_all | solution.py:41
  39.0 97.4 %copy-start.10 = (bf16[1,1,16,24,768]{4,3,2,1,0:T(8,128)(2,1)S(1)}, bf16[1,1,16,24,768]{4,3,2,1,0:T(8,128)(2,1)}, u32[]{:S(2)}) copy-start(bf16[1,1,16,24,768]{4,3,2,1,0:T(8,128)(2,1)} %get-tuple-element.12) | copy-start | bytes 1769476
  135.3 1.1 copy-start.7
  140.0 4.2 %copy-start.8 = (bf16[1,1,16,24,768]{4,3,2,1,0:T(8,128)(2,1)S(1)}, bf16[1,1,16,24,768]{4,3,2,1,0:T(8,128)(2,1)}, u32[]{:S(2)}) copy-start(bf16[1,1,16,24,768]{4,3,2,1,0:T(8,128)(2,1)} %get-tuple-element.11) | copy-start | bytes 1769476
  152.3 11.8 %all-to-all-start.1 = ((f32[4,16,24]{2,0,1:T(4,128)}), f32[4,16,24]{2,0,1:T(4,128)S(1)}, u32[]{:S(2)}, u32[]{:S(2)}) async-start(f32[4,16,24]{2,0,1:T(4,128)} %pad_maximum_fusion.2), calls=%async_computation.2 | async-start | bytes 65536 | tf_op jit(solution)/shard_map/all_to_all | solution.py:67
  157.7 218.8 %all-gather.3.cloned.1.call-start = ((), (), s32[]{:S(2)}) async-start(), calls=%async_computation.4 | async-start | bytes 67633152 | tf_op jit(solution)/shard_map/all_gather | solution.py:80
  164.3 6.5 %copy-start.13 = (f32[128,8]{0,1:T(8,128)S(1)}, f32[128,8]{0,1:T(8,128)}, u32[]{:S(2)}) copy-start(f32[128,8]{0,1:T(8,128)} %param.9) | copy-start | bytes 12292
  164.3 6.5 %copy-start.12 = (s32[128,8]{0,1:T(8,128)S(1)}, s32[128,8]{0,1:T(8,128)}, u32[]{:S(2)}) copy-start(s32[128,8]{0,1:T(8,128)} %param.10) | copy-start | bytes 12292
  171.9 226.4 %reduce-scatter.2.cloned.1.call-start = ((), (), s32[]{:S(2)}) async-start(), calls=%async_computation.3 | async-start | bytes 14155776 | tf_op jit(solution)/shard_map/reduce_scatter | solution.py:62
  172.1 3.6 copy-start.5
  172.1 3.5 copy-start.9
  175.7 1.9 copy-start.3
  187.4 3.9 copy-start.6
  191.3 3.4 copy-start.4
  201.7 1.7 copy-start.11
  376.6 21.7 %copy-start.1 = (bf16[128,2048]{1,0:T(8,128)(2,1)S(1)}, bf16[128,2048]{1,0:T(8,128)(2,1)}, u32[]{:S(2)}) copy-start(bf16[128,2048]{1,0:T(8,128)(2,1)} %param.7) | copy-start | bytes 1572868
Sparse Core Ops, SparseCore 0:
  172.0 204.5 all-gather.2
Sparse Core Ops, SparseCore 1:
  187.5 168.0 reduce-scatter.1
